TPU v7x, 256 devices: a whole 4x4x8 slice. The times are simulated.
256 devices in a mesh: wide: 16 (over x, y_lo, core), loop: 16 (over y_hi, z).
Axes of the slice: x: 4, y: 4 (y_hi: 2, y_lo: 2; y = y_hi * 2 + y_lo), z: 8, core: 2. Of those that a mesh axis runs over, the one named last changes fastest.
Arguments:
- query_grads: bfloat16 [65536, 16384], P('loop', 'wide'), may hold values from -6 to 6
- train_grads: bfloat16 [640, 16384], P('loop', 'wide'), may hold values from -0.046875 to 0.046875
- precond: bfloat16 [2048, 16384], P(None, 'wide'), may hold values from -3 to 3
Outputs:
- scores: float32 [65536, 640], P(('loop', 'wide'))
All inputs are finite; a program needn't handle non-finite values.
Results may differ from a plain program's by a relative error of at most 0.0029.
Values may be sent and summed in bfloat16 or wider, within the bound.
No kernel may reach another device: no remote copies, remote signals or barrier semaphores. Data moves between devices by JAX's collectives and lax.ppermute only.
A program may use at most 128 MiB of HBM per device.

v0:
```python
import jax
import jax.numpy as jnp
from jax import lax
from jax.sharding import PartitionSpec as P


def partner_2(block, axis, bit):
    count = lax.axis_size(axis)
    route = []
    for low in range(count):
        high = low | 1 << bit
        if high != low and high < count:
            route += [(low, high), (high, low)]
    return lax.ppermute(block, axis, route)


def contract_features(left_rows, right_rows):
    return lax.dot_general(
        left_rows, right_rows, (((1,), (1,)), ((), ())), preferred_element_type=jnp.float32
    )


def shards(query_grads, train_grads, precond):
    current = train_grads
    position = lax.axis_index("wide")
    partner = partner_2(current, "wide", 0)
    is_upper = position // 2**0 % 2
    current = jnp.where(
        is_upper == 1,
        jnp.concatenate([partner, current], axis=1),
        jnp.concatenate([current, partner], axis=1),
    )
    conditioned = jnp.dot(current, precond, preferred_element_type=jnp.float32).astype(jnp.bfloat16)
    owned_rows = lax.all_to_all(query_grads, "wide", split_axis=0, concat_axis=1, tiled=True)
    full_width = lax.all_gather(conditioned, "wide", axis=1, tiled=True)
    return contract_features(owned_rows, lax.all_gather(full_width, "loop", axis=0, tiled=True))


def solution(mesh):
    return jax.shard_map(
        shards,
        mesh=mesh,
        in_specs=(P("loop", "wide"), P("loop", "wide"), P(None, "wide")),
        out_specs=P(("loop", "wide"), None),
        check_vma=False,
    )
```

profile of v0, /device:TPU:1, one launch (start us, length us, event | category | flops | bytes accessed | tf_op | source)
XLA Modules:
  0.0 419.7 jit_solution(9244328703946631897)
XLA Ops:
  6.5 0.0 all-gather.3.cloned.1.call-start
  6.5 3.2 collective-permute-start
  9.8 1.1 collective-permute-done
  10.9 3.7 convolution_convert_fusion
  14.7 0.0 all-gather.3.cloned.1.call-update
  14.7 0.0 all-gather.5.cloned.1.call-start
  14.7 36.8 %all-gather.3.cloned.1.call-done = bf16[40,16384]{1,0:T(8,128)(2,1)} async-done(((bf16[40,1024]{1,0:T(8,128)(2,1)}), bf16[40,16384]{1,0:T(8,128)(2,1)}) %all-gather.3.cloned.1.call-update) | async-done | bytes 1310736 | tf_op jit(solution)/shard_map/all_gather | solution.py:35
  51.5 0.0 all-gather.5.cloned.1.call-update
  51.5 111.3 %all_to_all.19 = bf16[16,256,1024]{2,1,0:T(8,128)(2,1)} all-to-all(bf16[16,256,1024]{2,1,0:T(8,128)(2,1)} %bitcast.9), channel_id=1, replica_groups=mesh['wide'=16,'loop'=16] {'wide'}, dimensions={0} | all-to-all | bytes 16777216 | tf_op jit(solution)/shard_map/all_to_all | solution.py:34
  162.8 12.3 %copy.6 = bf16[256,16,1024]{0,2,1:T(8,128)(2,1)} copy(bf16[256,16,1024]{2,0,1:T(8,128)(2,1)} %bitcast.8) | data formatting | bytes 16777216 | tf_op jit(solution)/shard_map/all_to_all | solution.py:34
  175.1 224.4 %all-gather.5.cloned.1.call-done = bf16[640,16384]{1,0:T(8,128)(2,1)} async-done(((bf16[40,16384]{1,0:T(8,128)(2,1)}), bf16[640,16384]{1,0:T(8,128)(2,1)}) %all-gather.5.cloned.1.call-update) | async-done | bytes 20971536 | tf_op jit(solution)/shard_map/all_gather | solution.py:36
  399.5 12.2 %convolution_bitcast_fusion = f32[256,640]{0,1:T(8,128)S(1)} fusion(bf16[640,16384]{1,0:T(8,128)(2,1)} %all-gather.5.cloned.1.call-done, bf16[256,16384]{0,1:T(8,128)(2,1)} %bitcast.10), kind=kOutput, calls=%fused_computation | convolution fusion | flops 5368709120 | bytes 30015488 | tf_op jit(solution)/shard_map/dot_general | solution.py:18
  411.8 1.1 copy.7
Async XLA Ops:
  6.5 45.0 %all-gather.3.cloned.1.call-start = ((), (), s32[]{:S(2)}) async-start(), calls=%async_computation.1 | async-start | bytes 1392640 | tf_op jit(solution)/shard_map/all_gather | solution.py:35
  6.5 4.4 %collective-permute-start = (bf16[40,1024]{1,0:T(8,128)(2,1)}, bf16[40,1024]{1,0:T(8,128)(2,1)S(1)}, u32[]{:S(2)}, u32[]{:S(2)}) collective-permute-start(bf16[40,1024]{1,0:T(8,128)(2,1)} %param.4), channel_id=1, source_target_pairs={{0,16},{16,0},{32,48},{48,32},{64,80},{80,64},{96,112},{112,96},{1... | collective-permute-start | bytes 245768 | tf_op jit(solution)/shard_map/ppermute | solution.py:14
  14.7 384.9 %all-gather.5.cloned.1.call-start = ((), (), s32[]{:S(2)}) async-start(), calls=%async_computation.2 | async-start | bytes 22282240 | tf_op jit(solution)/shard_map/all_gather | solution.py:36
Sparse Core Ops, SparseCore 0:
  14.8 36.6 all-gather.2
  54.1 345.4 all-gather.4
where the time goes:
time: 420 us
  waiting for transfers between devices  262 us (62%)
  blocking collectives  111 us (26%)
  matrix products  16 us (4%)
  local copies, waits for them, and re-layouts  13.4 us (3%)
  between operations  13.4 us (3%)
    all_gather x1, waiting for transfers between devices, shards(): lax.all_gather(full_width, 'loop', axis=0, tiled=True)  224 us
    all_to_all x1, blocking collectives, shards(): lax.all_to_all(query_grads, 'wide', split_axis=0, concat_axis=1, tiled=True)  111 us
    all_gather x1, waiting for transfers between devices, shards(): full_width = lax.all_gather(conditioned, 'wide', axis=1, tiled=True)  36.8 us
    all_to_all x1, local copies, waits for them, and re-layouts, shards(): lax.all_to_all(query_grads, 'wide', split_axis=0, concat_axis=1, tiled=True)  12.3 us
    dot_general x1, matrix products, contract_features(): lax.dot_general(left_rows, right_rows, (((1,), (1,)), ((), ())), preferre...  12.2 us
  transfers between devices with their start and end apart: 3, of which 3 were waited for; matrix products, arithmetic and copies ran while one was open for 3% of the time, Pallas kernels for 0%

commit v1 on v0

--- a/solution.py
+++ b/solution.py
@@ -32,7 +32,14 @@
     )
     conditioned = jnp.dot(current, precond, preferred_element_type=jnp.float32).astype(jnp.bfloat16)
     owned_rows = lax.all_to_all(query_grads, "wide", split_axis=0, concat_axis=1, tiled=True)
-    full_width = lax.all_gather(conditioned, "wide", axis=1, tiled=True)
+
+    def map_the_floor(array_here, dev_axis, dim_no):
+        field_out = tuple((array_here for _ in range(lax.axis_size(dev_axis))))
+        n_now = jnp.stack(field_out, 0)
+        current_block = lax.all_to_all(n_now, axis_name=dev_axis, split_axis=0, concat_axis=0)
+        return jnp.concatenate(current_block, dim_no)
+
+    full_width = map_the_floor(conditioned, "wide", 1)
     return contract_features(owned_rows, lax.all_gather(full_width, "loop", axis=0, tiled=True))
 
 

time: 420 us -> 407 us (0.969)
  waiting for transfers between devices: 262 us -> 227 us
  blocking collectives: 111 us -> 134 us
    all_gather x1 -> x0, waiting for transfers between devices: 36.8 us -> none  [shards(): full_width = lax.all_gather(conditioned, 'wide', axis=1, tiled=True)]
    all_to_all x0 -> x1, blocking collectives: none -> 22.4 us  [map_the_floor(): lax.all_to_all(n_now, axis_name=dev_axis, split_axis=0, concat_axis=0)]
  transfers between devices with their start and end apart: 3 -> 2, of which waited for: 3 -> 2; matrix products, arithmetic and copies ran while one was open for 3% -> 3% of each run, Pallas kernels for 0% -> 0%
where the time goes in v1:
time: 407 us
  waiting for transfers between devices  227 us (56%)
  blocking collectives  134 us (33%)
  matrix products  15.3 us (4%)
  local copies, waits for them, and re-layouts  14.7 us (4%)
  between operations  13.4 us (3%)
    all_gather x1, waiting for transfers between devices, shards(): lax.all_gather(full_width, 'loop', axis=0, tiled=True)  225 us
    all_to_all x1, blocking collectives, shards(): lax.all_to_all(query_grads, 'wide', split_axis=0, concat_axis=1, tiled=True)  111 us
    all_to_all x1, blocking collectives, map_the_floor(): lax.all_to_all(n_now, axis_name=dev_axis, split_axis=0, concat_axis=0)  22.4 us
    all_to_all x1, local copies, waits for them, and re-layouts, shards(): lax.all_to_all(query_grads, 'wide', split_axis=0, concat_axis=1, tiled=True)  12.3 us
    dot_general x1, matrix products, contract_features(): lax.dot_general(left_rows, right_rows, (((1,), (1,)), ((), ())), preferre...  12.2 us
  transfers between devices with their start and end apart: 2, of which 2 were waited for; matrix products, arithmetic and copies ran while one was open for 3% of the time, Pallas kernels for 0%

profile of v1, /device:TPU:1, one launch (start us, length us, event | category | flops | bytes accessed | tf_op | source)
XLA Modules:
  0.0 407.0 jit_solution(10554240596947327090)
XLA Ops:
  6.5 0.0 all-gather.2.cloned.1.call-start
  6.5 3.2 collective-permute-start
  9.8 1.1 collective-permute-done
  10.9 3.1 convolution_convert_fusion
  14.0 0.1 stack.2
  14.2 22.4 %all_to_all.24 = bf16[16,40,1024]{2,1,0:T(8,128)(2,1)S(1)} all-to-all(bf16[16,40,1024]{2,1,0:T(8,128)(2,1)S(1)} %stack.2), channel_id=1, replica_groups=mesh['wide'=16,'loop'=16] {'wide'}, dimensions={0} | all-to-all | bytes 2621440 | tf_op jit(solution)/shard_map/all_to_all | solution.py:39
  36.6 1.2 copy.11
  37.7 0.0 all-gather.2.cloned.1.call-update
  37.8 111.4 %all_to_all.25 = bf16[16,256,1024]{2,1,0:T(8,128)(2,1)} all-to-all(bf16[16,256,1024]{2,1,0:T(8,128)(2,1)} %bitcast.12), channel_id=1, replica_groups=mesh['wide'=16,'loop'=16] {'wide'}, dimensions={0} | all-to-all | bytes 16777216 | tf_op jit(solution)/shard_map/all_to_all | solution.py:34
  149.2 12.3 %copy.9 = bf16[256,16,1024]{0,2,1:T(8,128)(2,1)} copy(bf16[256,16,1024]{2,0,1:T(8,128)(2,1)} %bitcast.11) | data formatting | bytes 16777216 | tf_op jit(solution)/shard_map/all_to_all | solution.py:34
  161.4 225.4 %all-gather.2.cloned.1.call-done = bf16[640,16384]{1,0:T(8,128)(2,1)} async-done(((bf16[40,16384]{1,0:T(8,128)(2,1)}), bf16[640,16384]{1,0:T(8,128)(2,1)}) %all-gather.2.cloned.1.call-update) | async-done | bytes 20971536 | tf_op jit(solution)/shard_map/all_gather | solution.py:43
  386.8 12.2 %convolution_bitcast_fusion = f32[256,640]{0,1:T(8,128)S(1)} fusion(bf16[640,16384]{1,0:T(8,128)(2,1)} %all-gather.2.cloned.1.call-done, bf16[256,16384]{0,1:T(8,128)(2,1)} %bitcast.13), kind=kOutput, calls=%fused_computation | convolution fusion | flops 5368709120 | bytes 30015488 | tf_op jit(solution)/shard_map/dot_general | solution.py:18
  399.1 1.1 copy.10
Async XLA Ops:
  6.5 380.3 %all-gather.2.cloned.1.call-start = ((), (), s32[]{:S(2)}) async-start(), calls=%async_computation.2 | async-start | bytes 22282240 | tf_op jit(solution)/shard_map/all_gather | solution.py:43
  6.5 4.4 %collective-permute-start = (bf16[40,1024]{1,0:T(8,128)(2,1)}, bf16[40,1024]{1,0:T(8,128)(2,1)S(1)}, u32[]{:S(2)}, u32[]{:S(2)}) collective-permute-start(bf16[40,1024]{1,0:T(8,128)(2,1)} %param.4), channel_id=1, source_target_pairs={{0,16},{16,0},{32,48},{48,32},{64,80},{80,64},{96,112},{112,96},{1... | collective-permute-start | bytes 245768 | tf_op jit(solution)/shard_map/ppermute | solution.py:14
Sparse Core Ops, SparseCore 0:
  37.9 348.8 all-gather.1

commit v2 on v0

--- a/solution.py
+++ b/solution.py
@@ -2,6 +2,14 @@
 import jax.numpy as jnp
 from jax import lax
 from jax.sharding import PartitionSpec as P
+
+
+def _push_vector(u, ax_name):
+    local_next = lax.axis_size(ax_name)
+    plain = jnp.split(u, local_next, 0)
+    all_values = jnp.stack(plain, axis=0)
+    small = lax.all_to_all(all_values, ax_name, 0, 0)
+    return jnp.concatenate(small, 1)
 
 
 def partner_2(block, axis, bit):
@@ -31,7 +39,7 @@
         jnp.concatenate([current, partner], axis=1),
     )
     conditioned = jnp.dot(current, precond, preferred_element_type=jnp.float32).astype(jnp.bfloat16)
-    owned_rows = lax.all_to_all(query_grads, "wide", split_axis=0, concat_axis=1, tiled=True)
+    owned_rows = _push_vector(query_grads, "wide")
     full_width = lax.all_gather(conditioned, "wide", axis=1, tiled=True)
     return contract_features(owned_rows, lax.all_gather(full_width, "loop", axis=0, tiled=True))
 

time: 420 us -> 396 us (0.943)
  waiting for transfers between devices: 262 us -> 215 us
  local copies, waits for them, and re-layouts: 13.4 us -> 37.6 us
    all_gather x1, waiting for transfers between devices: 224 us -> 177 us  [shards(): lax.all_gather(full_width, 'loop', axis=0, tiled=True)]
    unnamed x0 -> x37, local copies, waits for them, and re-layouts: none -> 31.8 us
    all_to_all x1 -> x0, local copies, waits for them, and re-layouts: 12.3 us -> none  [shards(): lax.all_to_all(query_grads, 'wide', split_axis=0, concat_axis=1, tiled=True)]
    split x0 -> x1, local copies, waits for them, and re-layouts: none -> 5.79 us  [_push_vector(): plain = jnp.split(u, local_next, 0)]
  transfers between devices with their start and end apart: 3 -> 3, of which waited for: 3 -> 3; matrix products, arithmetic and copies ran while one was open for 3% -> 10% of each run, Pallas kernels for 0% -> 0%
where the time goes in v2:
time: 396 us; the launch traced here: 395 us
  waiting for transfers between devices  215 us (54%)
  blocking collectives  108 us (27%)
  local copies, waits for them, and re-layouts  37.6 us (9%)
  matrix products  17.5 us (4%)
  between operations  13.6 us (3%)
    all_gather x1, waiting for transfers between devices, shards(): lax.all_gather(full_width, 'loop', axis=0, tiled=True)  177 us
    all_to_all x1, blocking collectives, _push_vector(): small = lax.all_to_all(all_values, ax_name, 0, 0)  108 us
    all_gather x1, waiting for transfers between devices, shards(): full_width = lax.all_gather(conditioned, 'wide', axis=1, tiled=True)  36.8 us
    unnamed x37, local copies, waits for them, and re-layouts  31.8 us
    dot_general x1, matrix products, contract_features(): lax.dot_general(left_rows, right_rows, (((1,), (1,)), ((), ())), preferre...  13.7 us
  transfers between devices with their start and end apart: 3, of which 3 were waited for; matrix products, arithmetic and copies ran while one was open for 10% of the time, Pallas kernels for 0%

profile of v2, /device:TPU:1, one launch (start us, length us, event | category | flops | bytes accessed | tf_op | source)
XLA Modules:
  0.0 395.2 jit_solution(902701439008302278)
XLA Ops:
  6.5 0.0 all-gather.3.cloned.1.call-start
  6.5 3.2 collective-permute-start
  9.8 1.1 collective-permute-done
  10.9 3.7 convolution_convert_fusion
  14.7 0.0 all-gather.3.cloned.1.call-update
  14.7 0.0 all-gather.5.cloned.1.call-start
  14.7 36.8 %all-gather.3.cloned.1.call-done = bf16[40,16384]{1,0:T(8,128)(2,1)} async-done(((bf16[40,1024]{1,0:T(8,128)(2,1)}), bf16[40,16384]{1,0:T(8,128)(2,1)}) %all-gather.3.cloned.1.call-update) | async-done | bytes 1310736 | tf_op jit(solution)/shard_map/all_gather | solution.py:43
  51.5 0.0 all-gather.5.cloned.1.call-update
  51.5 5.8 %fusion.7 = (bf16[256,1024]{1,0:T(8,128)(2,1)S(1)}, bf16[256,1024]{1,0:T(8,128)(2,1)S(1)}, bf16[256,1024]{1,0:T(8,128)(2,1)S(1)}, bf16[256,1024]{1,0:T(8,128)(2,...) fusion(bf16[4096,1024]{1,0:T(8,128)(2,1)} %param.3), kind=kLoop, calls=%fused_computation.25 | loop fusion | bytes 16777216 | tf_op jit(solution)/shard_map/split | solution.py:9
  57.3 2.1 copy.20
  59.4 2.1 copy.21
  61.4 2.1 copy.22
  63.5 2.0 copy.23
  65.5 2.1 copy.24
  67.7 2.1 copy.25
  69.8 2.1 copy.26
  71.9 2.0 copy.27
  74.0 2.0 copy.28
  76.0 2.0 copy.29
  78.1 1.0 copy.30
  79.1 0.2 copy.31
  79.3 0.2 copy.32
  79.5 0.2 copy.33
  79.7 0.2 copy.34
  79.9 0.2 copy.35
  80.1 0.0 copy-start.2
  80.1 0.0 copy-start.1
  80.1 0.0 copy-start
  80.1 1.2 bitcast_dynamic-update-slice_fusion.15
  81.3 1.1 bitcast_dynamic-update-slice_fusion.14
  82.4 1.1 bitcast_dynamic-update-slice_fusion.13
  83.5 1.1 bitcast_dynamic-update-slice_fusion.12
  84.6 1.1 bitcast_dynamic-update-slice_fusion.11
  85.7 1.1 bitcast_dynamic-update-slice_fusion.10
  86.7 1.1 bitcast_dynamic-update-slice_fusion.9
  87.8 1.1 bitcast_dynamic-update-slice_fusion.8
  88.9 0.0 copy-done.2
  89.0 0.0 copy-done.1
  89.0 0.0 copy-done
  89.3 108.0 %all_to_all.5 = bf16[16,256,1024]{1,2,0:T(8,128)(2,1)} all-to-all(bf16[16,256,1024]{1,2,0:T(8,128)(2,1)S(1)} %bitcast_dynamic-update-slice_fusion), channel_id=1, replica_groups=mesh['wide'=16,'loop'=16] {'wide'}, dimensions={0} | all-to-all | bytes 16777216 | tf_op jit(solution)/shard_map/all_to_all | solution.py:11
  197.4 177.3 %all-gather.5.cloned.1.call-done = bf16[640,16384]{1,0:T(8,128)(2,1)} async-done(((bf16[40,16384]{1,0:T(8,128)(2,1)}), bf16[640,16384]{1,0:T(8,128)(2,1)}) %all-gather.5.cloned.1.call-update) | async-done | bytes 20971536 | tf_op jit(solution)/shard_map/all_gather | solution.py:44
  374.7 13.7 %fusion.8 = f32[256,640]{1,0:T(8,128)} fusion(bf16[256,16384]{0,1:T(8,128)(2,1)} %bitcast.38, bf16[640,16384]{1,0:T(8,128)(2,1)} %all-gather.5.cloned.1.call-done), kind=kOutput, calls=%fused_computation.26 | convolution fusion | flops 5368709120 | bytes 30015488 | tf_op jit(solution)/shard_map/dot_general | solution.py:26
  (8 shorter events, 0.3 us)
Async XLA Ops:
  6.5 45.0 %all-gather.3.cloned.1.call-start = ((), (), s32[]{:S(2)}) async-start(), calls=%async_computation.1 | async-start | bytes 1392640 | tf_op jit(solution)/shard_map/all_gather | solution.py:43
  6.5 4.4 %collective-permute-start = (bf16[40,1024]{1,0:T(8,128)(2,1)}, bf16[40,1024]{1,0:T(8,128)(2,1)S(1)}, u32[]{:S(2)}, u32[]{:S(2)}) collective-permute-start(bf16[40,1024]{1,0:T(8,128)(2,1)} %param.4), channel_id=1, source_target_pairs={{0,16},{16,0},{32,48},{48,32},{64,80},{80,64},{96,112},{112,96},{1... | collective-permute-start | bytes 245768 | tf_op jit(solution)/shard_map/ppermute | solution.py:22
  14.7 360.0 %all-gather.5.cloned.1.call-start = ((), (), s32[]{:S(2)}) async-start(), calls=%async_computation.2 | async-start | bytes 22282240 | tf_op jit(solution)/shard_map/all_gather | solution.py:44
  80.1 8.8 %copy-start.2 = (bf16[256,1024]{0,1:T(8,128)(2,1)S(1)}, bf16[256,1024]{0,1:T(8,128)(2,1)}, u32[]{:S(2)}) copy-start(bf16[256,1024]{0,1:T(8,128)(2,1)} %copy.28) | copy-start | bytes 1572868
  80.1 8.9 %copy-start.1 = (bf16[256,1024]{0,1:T(8,128)(2,1)S(1)}, bf16[256,1024]{0,1:T(8,128)(2,1)}, u32[]{:S(2)}) copy-start(bf16[256,1024]{0,1:T(8,128)(2,1)} %copy.29) | copy-start | bytes 1572868
  80.1 8.9 %copy-start = (bf16[256,1024]{0,1:T(8,128)(2,1)S(1)}, bf16[256,1024]{0,1:T(8,128)(2,1)}, u32[]{:S(2)}) copy-start(bf16[256,1024]{0,1:T(8,128)(2,1)} %copy.30) | copy-start | bytes 1572868
Sparse Core Ops, SparseCore 0:
  14.8 36.6 all-gather.2
  54.1 320.5 all-gather.4
